TPU v7x, 32 devices: a whole 2x2x4 slice. The times are simulated.
32 devices in a mesh: loop: 8 (over z, core), red: 4 (over y, x).
Axes of the slice: x: 2, y: 2, z: 4, core: 2. Of those that a mesh axis runs over, the one named last changes fastest.
Arguments:
- query_ids: int32 [512], replicated, may hold values from 0 to 8191
- layer_index: int32 [1], replicated, may hold values from 0 to 3
- gradient: bfloat16 [8192, 28672], P('loop', 'red'), may hold values from -6 to 6
- out_basis: bfloat16 [8192, 8192], P('loop'), may hold values from -0.0625 to 0.0625
- in_basis: bfloat16 [28672, 28672], P('red', 'loop'), may hold values from -0.03125 to 0.03125
- out_eigen: float32 [4, 8192], replicated, may hold values from 0.2 to 2
- in_eigen: float32 [4, 28672], P(None, 'loop'), may hold values from 0.2 to 2
Outputs:
- preconditioned: bfloat16 [512, 28672], P('loop', 'red')
All inputs are finite; a program needn't handle non-finite values.
Results may differ from a plain program's by a relative error of at most 0.0055.
Values may be sent and summed in bfloat16 or wider, within the bound.
A program may use at most 192 MiB of HBM per device.

v0:
```python
import jax
import jax.numpy as jnp
from jax import lax
from jax.sharding import PartitionSpec as P

damping = 0.05


def per_device(query_ids, layer_index, gradient, out_basis, in_basis, out_eigen, in_eigen):
    selected = jnp.take(out_basis, query_ids, axis=1)
    shares = lax.psum_scatter(
        lax.dot_general(
            selected, gradient, (((0,), (0,)), ((), ())), preferred_element_type=jnp.float32
        ),
        "loop",
        scatter_dimension=0,
        tiled=True,
    )
    rows_w = lax.all_gather(shares.astype(jnp.bfloat16), "loop", axis=0, tiled=True)
    eigen_rows = jnp.take(jnp.take(out_eigen, layer_index, axis=0)[0], query_ids)
    eigen_cols = jnp.take(in_eigen, layer_index, axis=0)[0]
    local_rot = jnp.dot(rows_w, in_basis, preferred_element_type=jnp.float32)
    rotated = lax.psum(local_rot, "red")
    scaled = (rotated / (eigen_rows[:, None] * eigen_cols[None, :] + damping)).astype(jnp.bfloat16)
    result = lax.psum_scatter(
        lax.dot_general(
            scaled, in_basis, (((1,), (1,)), ((), ())), preferred_element_type=jnp.float32
        ),
        "loop",
        scatter_dimension=0,
        tiled=True,
    )
    return result.astype(jnp.bfloat16)


def solution(mesh):
    return jax.shard_map(
        per_device,
        mesh=mesh,
        in_specs=(
            P(),
            P(),
            P("loop", "red"),
            P("loop", None),
            P("red", "loop"),
            P(),
            P(None, "loop"),
        ),
        out_specs=P("loop", "red"),
        check_vma=False,
    )
```

profile of v0, /device:TPU:0, one launch (start us, length us, event | category | flops | bytes accessed | tf_op | source)
XLA Modules:
  0.0 673.3 jit_solution(5662324999065635593)
XLA Ops:
  6.5 0.0 reduce-scatter.3.cloned.1.call-start
  7.2 0.7 compare_select_fusion
  7.9 0.9 broadcast_select_fusion
  8.8 3.1 gather_fusion.1
  12.0 0.7 broadcast_select_fusion.2
  12.7 22.4 %copy.9 = bf16[1024,8192]{0,1:T(8,128)(2,1)} copy(bf16[1024,8192]{1,0:T(8,128)(2,1)} %param.10) | data formatting | bytes 33554432 | tf_op args[3]
  35.1 10.7 %gather_fusion = bf16[512,1024]{1,0:T(8,128)(2,1)S(1)} fusion(bf16[1024,8192]{0,1:T(8,128)(2,1)} %copy.9, s32[1024]{0:T(1024)S(1)} %pad_clamp_fusion), kind=kCustom, calls=%fused_computation | custom fusion | bytes 2099200 | tf_op jit(solution)/shard_map/jit(_take)/gather | solution.py:10
  45.8 16.3 %fusion.4 = f32[512,7168]{1,0:T(8,128)} fusion(bf16[1024,7168]{1,0:T(8,128)(2,1)} %param.9, bf16[512,1024]{1,0:T(8,128)(2,1)S(1)} %gather_fusion, pred[512]{0:T(512)(128)(4,1)S(1)} %get-tuple-element.28), kind=kOutput, calls=%fused_computation.7 | convolution fusion | flops 7516717056 | bytes 30409216 | tf_op jit(solution)/shard_map/dot_general | solution.py:12
  62.1 0.0 reduce-scatter.3.cloned.1.call-update
  62.1 0.0 all-gather.2.cloned.1.call-start
  62.2 151.8 %reduce-scatter.3.cloned.1.call-done = f32[64,7168]{1,0:T(8,128)} async-done(((f32[512,7168]{1,0:T(8,128)}), f32[64,7168]{1,0:T(8,128)}) %reduce-scatter.3.cloned.1.call-update) | async-done | bytes 1835024 | tf_op jit(solution)/shard_map/reduce_scatter | solution.py:11
  213.9 2.5 convert_element_type.9
  216.4 0.0 all-gather.2.cloned.1.call-update
  216.5 0.0 all-reduce.2.cloned.1.call-start
  216.5 71.9 %all-gather.2.cloned.1.call-done = bf16[512,7168]{1,0:T(8,128)(2,1)} async-done(((bf16[64,7168]{1,0:T(8,128)(2,1)}), bf16[512,7168]{1,0:T(8,128)(2,1)}) %all-gather.2.cloned.1.call-update) | async-done | bytes 7340048 | tf_op jit(solution)/shard_map/all_gather | solution.py:19
  288.5 35.4 %fusion.11 = f32[512,3584]{1,0:T(8,128)} fusion(bf16[512,7168]{1,0:T(8,128)(2,1)} %all-gather.2.cloned.1.call-done, bf16[7168,3584]{1,0:T(8,128)(2,1)} %param.11), kind=kOutput, calls=%fused_computation.20 | convolution fusion | flops 26306674688 | bytes 66060288 | tf_op jit(solution)/shard_map/dot_general | solution.py:22
  323.8 0.0 all-reduce.2.cloned.1.call-update
  323.9 0.2 reduce-scatter.5.cloned.1.call-start
  324.1 0.9 fusion.8
  325.0 153.0 %all-reduce.2.cloned.1.call-done = f32[512,3584]{1,0:T(8,128)} async-done(((f32[512,3584]{1,0:T(8,128)}), f32[512,3584]{1,0:T(8,128)}) %all-reduce.2.cloned.1.call-update) | async-done | bytes 7340048 | tf_op jit(solution)/shard_map/psum | solution.py:23
  478.0 37.1 %fusion = f32[512,7168]{1,0:T(8,128)} fusion(bf16[7168,3584]{1,0:T(8,128)(2,1)} %param.11, f32[512,3584]{1,0:T(8,128)} %all-reduce.2.cloned.1.call-done, f32[3584]{0:T(1024)S(1)} %fusion.8, f32[512]{0:T(512)S(1)} %get-tuple-element.27), kind=kOutput, calls=%fused_computation.3 | convolution fusion | flops 26314014720 | bytes 73416704 | tf_op jit(solution)/shard_map/dot_general | solution.py:26
  515.1 0.0 reduce-scatter.5.cloned.1.call-update
  515.2 149.1 %reduce-scatter.5.cloned.1.call-done = f32[64,7168]{1,0:T(8,128)} async-done(((f32[512,7168]{1,0:T(8,128)}), f32[64,7168]{1,0:T(8,128)}) %reduce-scatter.5.cloned.1.call-update) | async-done | bytes 1835024 | tf_op jit(solution)/shard_map/reduce_scatter | solution.py:25
  664.2 2.5 convert_element_type.11
  (1 shorter events, 0.0 us)
Async XLA Ops:
  6.5 207.4 %reduce-scatter.3.cloned.1.call-start = ((), (), s32[]{:S(2)}) async-start(), calls=%async_computation.2 | async-start | bytes 16515072 | tf_op jit(solution)/shard_map/reduce_scatter | solution.py:11
  62.1 226.3 %all-gather.2.cloned.1.call-start = ((), (), s32[]{:S(2)}) async-start(), calls=%async_computation.3 | async-start | bytes 8257536 | tf_op jit(solution)/shard_map/all_gather | solution.py:19
  216.5 261.5 %all-reduce.2.cloned.1.call-start = ((), (), s32[]{:S(2)}) async-start(), calls=%async_computation.4 | async-start | bytes 14680064 | tf_op jit(solution)/shard_map/psum | solution.py:23
  323.9 340.4 %reduce-scatter.5.cloned.1.call-start = ((), (), s32[]{:S(2)}) async-start(), calls=%async_computation.5 | async-start | bytes 16515072 | tf_op jit(solution)/shard_map/reduce_scatter | solution.py:25
Sparse Core Ops, SparseCore 0:
  62.2 151.6 reduce-scatter.2
  216.6 71.8 all-gather.1
  324.0 153.9 all-reduce.1
  515.3 148.9 reduce-scatter.4
where the time goes:
time: 674 us; the launch traced here: 673 us
  waiting for transfers between devices  526 us (78%)
  matrix products  88.8 us (13%)
  local copies, waits for them, and re-layouts  36.2 us (5%)
  between operations  13.8 us (2%)
  other arithmetic  8.23 us (1%)
    psum x1, waiting for transfers between devices, per_device(): rotated = lax.psum(local_rot, 'red')  153 us
    reduce_scatter x1, waiting for transfers between devices, per_device(): lax.psum_scatter(lax.dot_general(selected, gradient, (((0,), (0,)), ((),...  152 us
    reduce_scatter x1, waiting for transfers between devices, per_device(): lax.psum_scatter(lax.dot_general(scaled, in_basis, (((1,), (1,)), ((), ()...  149 us
    all_gather x1, waiting for transfers between devices, per_device(): lax.all_gather(shares.astype(jnp.bfloat16), 'loop', axis=0, tiled=True)  71.9 us
    dot_general x1, matrix products, per_device(): lax.dot_general(scaled, in_basis, (((1,), (1,)), ((), ())), preferred_ele...  37.1 us
    dot_general x1, matrix products, per_device(): local_rot = jnp.dot(rows_w, in_basis, preferred_element_type=jnp.float32)  35.4 us
    unnamed x1, local copies, waits for them, and re-layouts  22.4 us
    dot_general x1, matrix products, per_device(): lax.dot_general(selected, gradient, (((0,), (0,)), ((), ())), preferred_e...  16.3 us
  transfers between devices with their start and end apart: 4, of which 4 were waited for; matrix products, arithmetic and copies ran while one was open for 0% of the time, Pallas kernels for 0%

commit v1 on v0

--- a/solution.py
+++ b/solution.py
@@ -20,7 +20,9 @@
     eigen_rows = jnp.take(jnp.take(out_eigen, layer_index, axis=0)[0], query_ids)
     eigen_cols = jnp.take(in_eigen, layer_index, axis=0)[0]
     local_rot = jnp.dot(rows_w, in_basis, preferred_element_type=jnp.float32)
-    rotated = lax.psum(local_rot, "red")
+    rotated = local_rot
+    for hop in (1, 2):
+        rotated = rotated + lax.ppermute(rotated, "red", [(dev, dev ^ hop) for dev in range(4)])
     scaled = (rotated / (eigen_rows[:, None] * eigen_cols[None, :] + damping)).astype(jnp.bfloat16)
     result = lax.psum_scatter(
         lax.dot_general(

time: 674 us -> 852 us (1.26)
  waiting for transfers between devices: 526 us -> 686 us
    ppermute x0 -> x2, waiting for transfers between devices: none -> 314 us  [per_device(): lax.ppermute(rotated, 'red', [(dev, dev ^ hop) for dev in range(4)])]
    psum x1 -> x0, waiting for transfers between devices: 153 us -> none  [per_device(): rotated = lax.psum(local_rot, 'red')]
    unnamed x1 -> x7, local copies, waits for them, and re-layouts: 22.4 us -> 29.7 us
  transfers between devices with their start and end apart: 4 -> 5, of which waited for: 4 -> 5; matrix products, arithmetic and copies ran while one was open for 0% -> 0% of each run, Pallas kernels for 0% -> 0%
where the time goes in v1:
time: 852 us; the launch traced here: 851 us
  waiting for transfers between devices  686 us (81%)
  matrix products  90 us (11%)
  local copies, waits for them, and re-layouts  43.5 us (5%)
  other arithmetic  14.7 us (2%)
  between operations  13.8 us (2%)
    ppermute x2, waiting for transfers between devices, per_device(): lax.ppermute(rotated, 'red', [(dev, dev ^ hop) for dev in range(4)])  314 us
    reduce_scatter x1, waiting for transfers between devices, per_device(): lax.psum_scatter(lax.dot_general(selected, gradient, (((0,), (0,)), ((),...  152 us
    reduce_scatter x1, waiting for transfers between devices, per_device(): lax.psum_scatter(lax.dot_general(scaled, in_basis, (((1,), (1,)), ((), ()...  148 us
    all_gather x1, waiting for transfers between devices, per_device(): lax.all_gather(shares.astype(jnp.bfloat16), 'loop', axis=0, tiled=True)  71.8 us
    dot_general x1, matrix products, per_device(): lax.dot_general(scaled, in_basis, (((1,), (1,)), ((), ())), preferred_ele...  41 us
    dot_general x1, matrix products, per_device(): local_rot = jnp.dot(rows_w, in_basis, preferred_element_type=jnp.float32)  32.6 us
    unnamed x7, local copies, waits for them, and re-layouts  29.7 us
  transfers between devices with their start and end apart: 5, of which 5 were waited for; matrix products, arithmetic and copies ran while one was open for 0% of the time, Pallas kernels for 0%

profile of v1, /device:TPU:0, one launch (start us, length us, event | category | flops | bytes accessed | tf_op | source)
XLA Modules:
  0.0 850.8 jit_solution(2398677097094739325)
XLA Ops:
  6.5 0.0 reduce-scatter.3.cloned.1.call-start
  7.2 0.7 compare_select_fusion
  7.9 0.9 broadcast_select_fusion
  8.8 3.1 gather_fusion.1
  12.0 0.7 broadcast_select_fusion.2
  12.7 22.4 %copy.9 = bf16[1024,8192]{0,1:T(8,128)(2,1)} copy(bf16[1024,8192]{1,0:T(8,128)(2,1)} %param.10) | data formatting | bytes 33554432 | tf_op args[3]
  35.1 10.7 %gather_fusion = bf16[512,1024]{1,0:T(8,128)(2,1)S(1)} fusion(bf16[1024,8192]{0,1:T(8,128)(2,1)} %copy.9, s32[1024]{0:T(1024)S(1)} %pad_clamp_fusion), kind=kCustom, calls=%fused_computation | custom fusion | bytes 2099200 | tf_op jit(solution)/shard_map/jit(_take)/gather | solution.py:10
  45.8 16.3 %fusion.4 = f32[512,7168]{1,0:T(8,128)} fusion(bf16[1024,7168]{1,0:T(8,128)(2,1)} %param.9, bf16[512,1024]{1,0:T(8,128)(2,1)S(1)} %gather_fusion, pred[512]{0:T(512)(128)(4,1)S(1)} %get-tuple-element.28), kind=kOutput, calls=%fused_computation.7 | convolution fusion | flops 7516717056 | bytes 30409216 | tf_op jit(solution)/shard_map/dot_general | solution.py:12
  62.1 0.0 reduce-scatter.3.cloned.1.call-update
  62.1 0.0 all-gather.2.cloned.1.call-start
  62.2 151.8 %reduce-scatter.3.cloned.1.call-done = f32[64,7168]{1,0:T(8,128)} async-done(((f32[512,7168]{1,0:T(8,128)}), f32[64,7168]{1,0:T(8,128)}) %reduce-scatter.3.cloned.1.call-update) | async-done | bytes 1835024 | tf_op jit(solution)/shard_map/reduce_scatter | solution.py:11
  213.9 2.5 convert_element_type.9
  216.4 0.0 all-gather.2.cloned.1.call-update
  216.5 0.2 reduce-scatter.5.cloned.1.call-start
  216.7 71.8 %all-gather.2.cloned.1.call-done = bf16[512,7168]{1,0:T(8,128)(2,1)} async-done(((bf16[64,7168]{1,0:T(8,128)(2,1)}), bf16[512,7168]{1,0:T(8,128)(2,1)}) %all-gather.2.cloned.1.call-update) | async-done | bytes 7340048 | tf_op jit(solution)/shard_map/all_gather | solution.py:19
  288.5 32.6 %fusion.11 = f32[512,3584]{1,0:T(8,128)S(1)} fusion(bf16[512,7168]{1,0:T(8,128)(2,1)} %all-gather.2.cloned.1.call-done, bf16[7168,3584]{1,0:T(8,128)(2,1)} %param.11), kind=kOutput, calls=%fused_computation.20 | convolution fusion | flops 26306674688 | bytes 66060288 | tf_op jit(solution)/shard_map/dot_general | solution.py:22
  321.1 0.0 copy-start.1
  321.1 1.5 collective-permute-start
  322.7 1.4 copy-done.1
  324.1 157.4 %collective-permute-done = f32[512,3584]{1,0:T(8,128)} collective-permute-done((f32[512,3584]{1,0:T(8,128)S(1)}, f32[512,3584]{1,0:T(8,128)}, u32[]{:S(2)}, u32[]{:S(2)}) %collective-permute-start) | collective-permute-done | bytes 7340064 | tf_op jit(solution)/shard_map/ppermute | solution.py:25
  481.4 6.5 add.36
  487.9 0.0 copy-start
  487.9 2.9 copy-done
  490.8 1.5 collective-permute-start.1
  492.3 0.9 fusion.8
  493.2 156.9 %collective-permute-done.1 = f32[512,3584]{1,0:T(8,128)S(1)} collective-permute-done((f32[512,3584]{1,0:T(8,128)S(1)}, f32[512,3584]{1,0:T(8,128)S(1)}, u32[]{:S(2)}, u32[]{:S(2)}) %collective-permute-start.1) | collective-permute-done | bytes 7340064 | tf_op jit(solution)/shard_map/ppermute | solution.py:25
  650.1 0.0 copy-start.2
  650.1 2.9 copy-done.2
  653.1 41.0 %fusion = f32[512,7168]{1,0:T(8,128)} fusion(bf16[7168,3584]{1,0:T(8,128)(2,1)} %param.11, f32[512,3584]{1,0:T(8,128)} %copy-done, f32[512,3584]{1,0:T(8,128)} %copy-done.2, f32[3584]{0:T(1024)S(1)} %fusion.8, f32[512]{0:T(512)S(1)} %get-tuple-element.27), kind=kOutput, calls=%fused_computation.3 | convolution fusion | flops 26315849728 | bytes 80756736 | tf_op jit(solution)/shard_map/dot_general | solution.py:28
  694.0 0.0 reduce-scatter.5.cloned.1.call-update
  694.1 147.7 %reduce-scatter.5.cloned.1.call-done = f32[64,7168]{1,0:T(8,128)} async-done(((f32[512,7168]{1,0:T(8,128)}), f32[64,7168]{1,0:T(8,128)}) %reduce-scatter.5.cloned.1.call-update) | async-done | bytes 1835024 | tf_op jit(solution)/shard_map/reduce_scatter | solution.py:27
  841.7 2.5 convert_element_type.11
  (1 shorter events, 0.0 us)
Async XLA Ops:
  6.5 207.4 %reduce-scatter.3.cloned.1.call-start = ((), (), s32[]{:S(2)}) async-start(), calls=%async_computation.2 | async-start | bytes 16515072 | tf_op jit(solution)/shard_map/reduce_scatter | solution.py:11
  62.1 226.3 %all-gather.2.cloned.1.call-start = ((), (), s32[]{:S(2)}) async-start(), calls=%async_computation.3 | async-start | bytes 8257536 | tf_op jit(solution)/shard_map/all_gather | solution.py:19
  216.5 625.3 %reduce-scatter.5.cloned.1.call-start = ((), (), s32[]{:S(2)}) async-start(), calls=%async_computation.4 | async-start | bytes 16515072 | tf_op jit(solution)/shard_map/reduce_scatter | solution.py:27
  321.1 3.0 copy-start.1
  321.1 160.3 %collective-permute-start = (f32[512,3584]{1,0:T(8,128)S(1)}, f32[512,3584]{1,0:T(8,128)}, u32[]{:S(2)}, u32[]{:S(2)}) collective-permute-start(f32[512,3584]{1,0:T(8,128)S(1)} %fusion.11), channel_id=1, source_target_pairs={{0,1},{1,0},{2,3},{3,2},{4,5},{5,4},{6,7},{7,6},{8,9},{9,8},{10,11... | collective-permute-start | bytes 22020104 | tf_op jit(solution)/shard_map/ppermute | solution.py:25
  487.9 2.9 copy-start
  490.8 159.3 %collective-permute-start.1 = (f32[512,3584]{1,0:T(8,128)S(1)}, f32[512,3584]{1,0:T(8,128)S(1)}, u32[]{:S(2)}, u32[]{:S(2)}) collective-permute-start(f32[512,3584]{1,0:T(8,128)S(1)} %add.36), channel_id=1, source_target_pairs={{0,2},{1,3},{2,0},{3,1},{4,6},{5,7},{6,4},{7,5},{8,10},{9,11},{10,... | collective-permute-start | bytes 22020104 | tf_op jit(solution)/shard_map/ppermute | solution.py:25
  650.1 3.0 copy-start.2
Sparse Core Ops, SparseCore 0:
  62.2 151.6 reduce-scatter.2
  216.6 71.8 all-gather.1
  694.2 147.4 reduce-scatter.4
